TPU v7x, 32 devices: a whole 2x2x4 slice. The times are simulated.
32 devices in a mesh: row: 4 (over y, core), col: 8 (over z, x).
Axes of the slice: x: 2, y: 2, z: 4, core: 2. Of those that a mesh axis runs over, the one named last changes fastest.
Arguments:
- elem_residual: bfloat16 [16384, 3, 256], P(('row', 'col')), may hold values from -6 to 6
- corners: int32 [16384, 3], P(('row', 'col')), may hold values from 0 to 383
- share_rows: int32 [32, 2, 64], P(('row', 'col')), may hold values from 0 to 255
- x_factor: bfloat16 [8192, 1728], P(('row', 'col')), may hold values from -0.40039062 to 0.40039062, as said below
Outputs:
- solution: float32 [8192, 256], P(('row', 'col'))
Inputs may be any that keep to these rules, and one draw needn't show every extreme that they name: `corners`: values below 256 are own vertices, the next 64 the slots shared with the left neighbour, the last 64 those shared with the right neighbour. `share_rows`: own row indices; a row may appear several times. `x_factor`: independent entries, each column block with its own scale.
All inputs are finite; a program needn't handle non-finite values.
Results may differ from a plain program's by a relative error of at most 0.0035.
Values sent between devices are 32-bit elements; how exact they have to be, the bound alone decides.
A program may use at most 64 MiB of HBM per device.

v0:
```python
import functools

import jax
import jax.numpy as jnp
from jax import lax
from jax.experimental import pallas as pl
from jax.experimental.pallas import tpu as pltpu
from jax.sharding import PartitionSpec as P

INNER = 1408
MESH = pl.DeviceIdType.MESH
F32 = jnp.float32
BF16 = jnp.bfloat16


def swapped(block, axis, stride):
    count = lax.axis_size(axis)
    route = []
    for low in range(count):
        high = low | 1 << stride
        if high != low and high < count:
            route += [(low, high), (high, low)]
    return lax.ppermute(block, axis, route)


def summed_levels(blocks, n_row, n_col):
    col_bits = n_col.bit_length() - 1
    row_bits = n_row.bit_length() - 1
    for bit in range(col_bits + row_bits):
        axis, stride = ("col", bit) if bit < col_bits else ("row", bit - col_bits)
        partner = swapped(blocks[bit:], axis, stride)
        blocks = jnp.concatenate([blocks[:bit], blocks[bit:] + partner], axis=0)
    return blocks


def by_rounds(n_row, n_col, elem_residual, corners, share_rows, x_factor):
    rows_dev = x_factor.shape[0]
    shared = share_rows.shape[2]
    width = elem_residual.shape[2]
    levels = (n_row * n_col).bit_length() - 1
    ext_len = rows_dev + 2 * shared
    flat_ids = corners.reshape(-1)
    onehot = (
        lax.broadcasted_iota(jnp.int32, (ext_len, flat_ids.shape[0]), 0) == flat_ids[None, :]
    ).astype(BF16)
    extended = jnp.dot(onehot, elem_residual.reshape(-1, width), preferred_element_type=F32)
    forward = [(i, (i + 1) % n_col) for i in range(n_col)]
    backward = [(target, source) for source, target in forward]
    from_left = lax.ppermute(extended[rows_dev + shared :], "col", forward)
    from_right = lax.ppermute(extended[rows_dev : rows_dev + shared], "col", backward)
    row_ids = lax.broadcasted_iota(jnp.int32, (rows_dev, shared), 0)
    assembled = extended[:rows_dev]
    for side, received in ((0, from_left), (1, from_right)):
        side_map = (row_ids == share_rows[0, side][None, :]).astype(F32)
        assembled = assembled + jnp.dot(
            side_map, received, precision=lax.Precision.HIGHEST, preferred_element_type=F32
        )
    partial_value = lax.dot_general(
        x_factor, assembled.astype(BF16), (((0,), (0,)), ((), ())), preferred_element_type=F32
    )
    blocks = partial_value[INNER:].reshape(levels, -1, width)
    blocks = summed_levels(blocks, n_row, n_col)
    coef = jnp.concatenate([partial_value[:INNER], blocks.reshape(-1, width)], axis=0)
    return jnp.dot(x_factor, coef.astype(BF16), preferred_element_type=F32)


class Plan:
    def __init__(self, n_row, n_col, sep):
        self.n_row, self.n_col, self.sep = n_row, n_col, sep
        self.levels = (n_row * n_col).bit_length() - 1
        self.col_bits = n_col.bit_length() - 1
        self.groups = []
        if self.levels > self.col_bits:
            self.groups += [(level, level) for level in range(self.levels, self.col_bits, -1)]
        self.groups += [(level, level) for level in range(self.col_bits, 1, -1)]

    def span(self, level):
        return min(2**level, self.n_col)

    def row_span(self, level):
        return max(1, 2**level // self.n_col)

    def piece(self, level):
        return self.sep // self.span(level)


def takes(n_row, n_col, sep):
    return n_col >= 4 and 2 <= n_row <= 4 and sep % (8 * n_col) == 0


def tdot(a, b):
    return lax.dot_general(a, b, (((0,), (0,)), ((), ())), preferred_element_type=F32)


def kernel(
    plan,
    er_hbm, cor_hbm, sh_hbm, x_hbm,
    out_ref,
    er, cor, sh, xt,
    halo_out, halo_in, own, rhs, part, l1_in, rs_in, ex_out, ex_in, final, turned,
    in_sem, halo_s, halo_r, l1_s, l1_r, rs_s, rs_r, ex_s, ex_r, ag_s, ag_r,
):
    row, col = lax.axis_index("row"), lax.axis_index("col")
    levels, n_col = plan.levels, plan.n_col
    rows_dev = out_ref.shape[0]
    shared = halo_out.shape[1]
    kinds = er.shape[0]
    elems = er.shape[1]
    inner = xt.shape[0] - plan.sep * levels

    right = (row, (col + 1) % n_col)
    left = (row, (col + n_col - 1) % n_col)

    def col_peer(span, m):
        local = col % span
        return (row, col - local + (local + m) % span)

    def row_peer(span, k):
        local = row % span
        return (row - local + (local + k) % span, col)

    greeted = [col_peer(n_col, m) for m in range(1, n_col)]
    greeted += [row_peer(plan.n_row, k) for k in range(1, plan.n_row)]
    barrier = pltpu.get_barrier_semaphore()
    for peer in greeted:
        pl.semaphore_signal(barrier, inc=1, device_id=peer, device_id_type=MESH)

    loads = [
        pltpu.make_async_copy(source, target, in_sem.at[i])
        for i, (source, target) in enumerate(
            ((cor_hbm, cor), (er_hbm, er), (sh_hbm, sh), (x_hbm, xt))
        )
    ]
    for load in loads:
        load.start()

    def assembled_rows(start, count):
        total = None
        for k in range(kinds):
            ids = cor[k : k + 1, :]
            at = lax.broadcasted_iota(jnp.int32, (count, elems), 0) + start
            onehot = jnp.where(at == ids, 1.0, 0.0).astype(BF16)
            term = jnp.dot(onehot, er[k], preferred_element_type=F32)
            total = term if total is None else total + term
        return total

    loads[0].wait()
    loads[1].wait()
    halo_out[...] = assembled_rows(rows_dev, 2 * shared).reshape(halo_out.shape)
    own[...] = assembled_rows(0, rows_dev)
    pl.semaphore_wait(barrier, len(greeted))

    def remote(source, target, send, recv, peer):
        copy = pltpu.make_async_remote_copy(
            src_ref=source,
            dst_ref=target,
            send_sem=send,
            recv_sem=recv,
            device_id=peer,
            device_id_type=MESH,
        )
        copy.start()
        return copy

    sent = []
    halo = [
        remote(halo_out.at[1], halo_in.at[0], halo_s.at[0], halo_r.at[0], right),
        remote(halo_out.at[0], halo_in.at[1], halo_s.at[1], halo_r.at[1], left),
    ]
    sent += halo

    loads[2].wait()
    targets = jnp.concatenate([sh[0:1, :], sh[1:2, :]], axis=1)
    at = lax.broadcasted_iota(jnp.int32, (rows_dev, 2 * shared), 0)
    share_map = jnp.where(at == targets, 1.0, 0.0).astype(BF16)
    share_map = jnp.concatenate([share_map, share_map], axis=1)
    loads[3].wait()
    for copy in halo:
        copy.wait_recv()
    received = halo_in[...].reshape(2 * shared, -1)
    high = received.astype(BF16)
    low = (received - high.astype(F32)).astype(BF16)
    received = jnp.concatenate([high, low], axis=0)
    assembled = own[...] + jnp.dot(share_map, received, preferred_element_type=F32)
    rhs[...] = assembled.astype(BF16)

    def partial(low, high):
        rows = xt[inner + plan.sep * (low - 1) : inner + plan.sep * high, :]
        block = jnp.dot(rows, rhs[...], preferred_element_type=F32)
        part[low - 1 : high] = block.reshape(high - low + 1, plan.sep, -1)


    def own_rows(level, ahead=0):
        span, rows = plan.span(level), plan.piece(level)
        return pl.ds(pl.multiple_of((col % span + ahead) % span * rows, 8), rows)

    rs, ex, ag = {}, {}, {}
    def scatter(low, high):
        count = high - low + 1
        for m in range(1, plan.span(low)):
            rs[low, m] = remote(
                part.at[pl.ds(low - 1, count), own_rows(low, m)],
                rs_in.at[m - 1, pl.ds(low - 1, count), pl.ds(0, plan.piece(low))],
                rs_s.at[low - 1, m - 1],
                rs_r.at[low - 1, m - 1],
                col_peer(plan.span(low), m),
            )
    partial(plan.col_bits + 1, levels)
    for group in plan.groups:
        if group[0] > plan.col_bits:
            scatter(*group)
    partial(1, plan.col_bits)
    weights = jnp.dot(xt[:inner, :], rhs[...], preferred_element_type=F32).astype(BF16)
    out_ref[...] = tdot(xt[:inner, :], weights)
    for group in plan.groups:
        if group[0] <= plan.col_bits:
            scatter(*group)
    turned[...] = xt[inner:, :].T
    sent += list(rs.values())

    def gather(low, high):
        count = high - low + 1
        block = final.at[pl.ds(low - 1, count), own_rows(low)]
        for m in range(1, plan.span(low)):
            ag[low, m] = remote(
                block,
                block,
                ag_s.at[low - 1, m - 1],
                ag_r.at[low - 1, m - 1],
                col_peer(plan.span(low), m),
            )

    for low, high in plan.groups:
        rows = plan.piece(low)
        for m in range(1, plan.span(low)):
            rs[low, m].wait_recv()
        for level in range(low, high + 1):
            total = part[level - 1, own_rows(level)]
            for m in range(1, plan.span(low)):
                total = total + rs_in[m - 1, level - 1, pl.ds(0, rows)]
            if level <= plan.col_bits:
                final[level - 1, own_rows(level)] = total
            else:
                ex_out[level - plan.col_bits - 1] = total
        if low <= plan.col_bits:
            gather(low, high)
            continue
        for k in range(1, plan.n_row):
            for level in range(low, high + 1):
                if k < plan.row_span(level):
                    at_level = level - plan.col_bits - 1
                    ex[level, k] = remote(
                        ex_out.at[at_level],
                        ex_in.at[at_level, k - 1],
                        ex_s.at[at_level, k - 1],
                        ex_r.at[at_level, k - 1],
                        row_peer(plan.row_span(level), k),
                    )
    first = remote(part.at[0], l1_in, l1_s.at[0], l1_r.at[0], col_peer(2, 1))
    sent += list(ex.values()) + [first]
    if plan.levels > plan.col_bits:
        low, high = plan.col_bits + 1, levels
        for level in range(low, high + 1):
            at_level = level - plan.col_bits - 1
            total = ex_out[at_level]
            for k in range(1, plan.row_span(level)):
                ex[level, k].wait_recv()
                total = total + ex_in[at_level, k - 1]
            final[level - 1, own_rows(level)] = total
            gather(level, level)
    sent += list(ag.values())

    def applied(low, high):
        coef = final[low - 1 : high].reshape(plan.sep * (high - low + 1), -1).astype(BF16)
        return jnp.dot(turned[:, plan.sep * (low - 1) : plan.sep * high], coef, preferred_element_type=F32)

    first.wait_recv()
    final[0] = part[0] + l1_in[...]
    for (low, m), copy in ag.items():
        if low <= plan.col_bits:
            copy.wait_recv()
    out_ref[...] += applied(1, plan.col_bits)
    for (low, m), copy in ag.items():
        if low > plan.col_bits:
            copy.wait_recv()
    out_ref[...] += applied(plan.col_bits + 1, levels)
    for copy in sent:
        copy.wait_send()


def in_one_kernel(plan, elem_residual, corners, share_rows, x_factor):
    rows_dev, cols = x_factor.shape
    shared = share_rows.shape[2]
    elems, kinds, width = elem_residual.shape
    levels, sep = plan.levels, plan.sep
    slots = plan.n_col - 1
    row_levels = levels - plan.col_bits
    row_slots = plan.n_row - 1
    half = sep // 4
    small = sep // plan.n_col
    dma = pltpu.SemaphoreType.DMA
    anywhere = pl.BlockSpec(memory_space=pl.ANY)
    return pl.pallas_call(
        functools.partial(kernel, plan),
        out_shape=pltpu.VMEM((rows_dev, width), F32),
        in_specs=[anywhere] * 4,
        out_specs=pl.BlockSpec(memory_space=pltpu.VMEM),
        scratch_shapes=[
            pltpu.VMEM((kinds, elems, width), BF16),
            pltpu.VMEM((kinds, elems), jnp.int32),
            pltpu.VMEM((2, shared), jnp.int32),
            pltpu.VMEM((cols, rows_dev), BF16),
            pltpu.VMEM((2, shared, width), F32),
            pltpu.VMEM((2, shared, width), F32),
            pltpu.VMEM((rows_dev, width), F32),
            pltpu.VMEM((rows_dev, width), BF16),
            pltpu.VMEM((levels, sep, width), F32),
            pltpu.VMEM((sep, width), F32),
            pltpu.VMEM((slots, levels, half, width), F32),
            pltpu.VMEM((row_levels, small, width), F32),
            pltpu.VMEM((row_levels, row_slots, small, width), F32),
            pltpu.VMEM((levels, sep, width), F32),
            pltpu.VMEM((rows_dev, sep * levels), BF16),
            dma((4,)),
            dma((2,)),
            dma((2,)),
            dma((1,)),
            dma((1,)),
            dma((levels, slots)),
            dma((levels, slots)),
            dma((row_levels, row_slots)),
            dma((row_levels, row_slots)),
            dma((levels, slots)),
            dma((levels, slots)),
        ],
        compiler_params=pltpu.CompilerParams(collective_id=0, has_side_effects=True),
        name="factor_solve",
    )(
        elem_residual.transpose(1, 0, 2),
        corners.T,
        share_rows.reshape(2, shared),
        x_factor.T,
    )


def solution(mesh):
    n_row, n_col = mesh.shape["row"], mesh.shape["col"]
    levels = (n_row * n_col).bit_length() - 1

    def per_device(elem_residual, corners, share_rows, x_factor):
        sep = (x_factor.shape[1] - INNER) // levels
        args = (elem_residual, corners, share_rows, x_factor)
        if takes(n_row, n_col, sep):
            return in_one_kernel(Plan(n_row, n_col, sep), *args)
        return by_rounds(n_row, n_col, *args)

    placed = (
        P(("row", "col"), None, None),
        P(("row", "col"), None),
        P(("row", "col"), None, None),
        P(("row", "col"), None),
    )
    return jax.shard_map(
        per_device, mesh=mesh, in_specs=placed, out_specs=P(("row", "col"), None), check_vma=False
    )
```

profile of v0, /device:TPU:0, one launch (start us, length us, event | category | flops | bytes accessed | tf_op | source)
XLA Modules:
  0.0 25.5 jit_solution(12399524987916199416)
XLA Ops:
  0.0 24.8 %factor_solve.1 = f32[256,256]{1,0:T(8,128)S(1)} custom-call(bf16[3,512,256]{2,1,0:T(8,128)(2,1)} %bitcast.5, s32[3,512]{1,0:T(4,128)} %bitcast.6, s32[2,64]{1,0:T(2,128)} %bitcast.7, bf16[1728,256]{1,0:T(8,128)(2,1)} %bitcast.4), custom_call_target="tpu_custom_call" | custom-call | tf_op jit(solution)/shard_map/factor_solve/pallas_call | solution.py:303
  24.8 0.7 %copy.6 = f32[256,256]{1,0:T(8,128)} copy(f32[256,256]{1,0:T(8,128)S(1)} %factor_solve.1) | data formatting | bytes 524288
where the time goes:
time: 25.7 us; the launch traced here: 25.5 us
  Pallas kernels  24.8 us (96%)
  local copies, waits for them, and re-layouts  0.71 us (3%)
    pallas_call x1, Pallas kernels, in_one_kernel(): pl.pallas_call(functools.partial(kernel, plan), out_shape=pltpu.VMEM((row...  24.8 us
    unnamed x1, local copies, waits for them, and re-layouts  0.71 us

commit v1 on v0

v1 whole, which is shorter than its diff:
```python
import functools

import jax
import jax.numpy as jnp
from jax import lax
from jax.experimental import pallas as pl
from jax.experimental.pallas import tpu as pltpu
from jax.sharding import PartitionSpec as P

INNER = 1408
MESH = pl.DeviceIdType.MESH
F32 = jnp.float32
BF16 = jnp.bfloat16


def swapped(block, axis, stride):
    count = lax.axis_size(axis)
    route = []
    for low in range(count):
        high = low | 1 << stride
        if high != low and high < count:
            route += [(low, high), (high, low)]
    return lax.ppermute(block, axis, route)


def summed_levels(blocks, n_row, n_col):
    col_bits = n_col.bit_length() - 1
    row_bits = n_row.bit_length() - 1
    for bit in range(col_bits + row_bits):
        axis, stride = ("col", bit) if bit < col_bits else ("row", bit - col_bits)
        partner = swapped(blocks[bit:], axis, stride)
        blocks = jnp.concatenate([blocks[:bit], blocks[bit:] + partner], axis=0)
    return blocks


def by_rounds(n_row, n_col, elem_residual, corners, share_rows, x_factor):
    rows_dev = x_factor.shape[0]
    shared = share_rows.shape[2]
    width = elem_residual.shape[2]
    levels = (n_row * n_col).bit_length() - 1
    ext_len = rows_dev + 2 * shared
    flat_ids = corners.reshape(-1)
    onehot = (
        lax.broadcasted_iota(jnp.int32, (ext_len, flat_ids.shape[0]), 0) == flat_ids[None, :]
    ).astype(BF16)
    extended = jnp.dot(onehot, elem_residual.reshape(-1, width), preferred_element_type=F32)
    forward = [(i, (i + 1) % n_col) for i in range(n_col)]
    backward = [(target, source) for source, target in forward]
    from_left = lax.ppermute(extended[rows_dev + shared :], "col", forward)
    from_right = lax.ppermute(extended[rows_dev : rows_dev + shared], "col", backward)
    row_ids = lax.broadcasted_iota(jnp.int32, (rows_dev, shared), 0)
    assembled = extended[:rows_dev]
    for side, received in ((0, from_left), (1, from_right)):
        side_map = (row_ids == share_rows[0, side][None, :]).astype(F32)
        assembled = assembled + jnp.dot(
            side_map, received, precision=lax.Precision.HIGHEST, preferred_element_type=F32
        )
    partial_value = lax.dot_general(
        x_factor, assembled.astype(BF16), (((0,), (0,)), ((), ())), preferred_element_type=F32
    )
    blocks = partial_value[INNER:].reshape(levels, -1, width)
    blocks = summed_levels(blocks, n_row, n_col)
    coef = jnp.concatenate([partial_value[:INNER], blocks.reshape(-1, width)], axis=0)
    return jnp.dot(x_factor, coef.astype(BF16), preferred_element_type=F32)


class Plan:
    def __init__(self, n_row, n_col, sep):
        self.n_row, self.n_col, self.sep = n_row, n_col, sep
        self.levels = (n_row * n_col).bit_length() - 1
        self.col_bits = n_col.bit_length() - 1
        self.wide = list(range(self.levels, self.col_bits - 1, -1))
        self.narrow = list(range(self.col_bits - 1, 1, -1))

    def row_span(self, level):
        return max(1, 2**level // self.n_col)

    def row_step(self, level):
        return self.n_col // 2 * self.row_span(level) // self.n_owners(level)

    def n_owners(self, level):
        return min(self.n_col // 2 * self.row_span(level), self.sep // 8)

    def piece(self, level):
        return self.sep // self.n_owners(level)

    def owners(self, level):
        rows = range(0, self.row_span(level), self.row_step(level))
        return [(r, self.n_col // 4 + c) for r in rows for c in range(self.n_col // 2)]

    def members(self, level):
        every = [(r, c) for r in range(self.row_span(level)) for c in range(self.n_col)]
        return sorted(every, key=lambda at: (at[1] // 2, at[0] % 2, at[1], at[0]))


def takes(n_row, n_col, sep):
    return n_col >= 4 and 2 <= n_row <= 4 and sep % (8 * n_col) == 0


def tdot(a, b):
    return lax.dot_general(a, b, (((0,), (0,)), ((), ())), preferred_element_type=F32)


def kernel(
    plan,
    er_hbm, cor_hbm, sh_hbm, x_hbm,
    out_ref,
    er, cor, sh, xt,
    halo_out, halo_in, own, rhs, part, l1_in, near_in, final, turned,
    in_sem, halo_s, halo_r, l1_s, l1_r, near_s, near_r, near_gs, near_gr, wide_s, wide_r, ag_s, ag_r,
    *wide_in,
):
    row, col = lax.axis_index("row"), lax.axis_index("col")
    levels, n_row, n_col, sep = plan.levels, plan.n_row, plan.n_col, plan.sep
    rows_dev = out_ref.shape[0]
    shared = halo_out.shape[1]
    kinds = er.shape[0]
    elems = er.shape[1]
    inner = xt.shape[0] - sep * levels
    wide_in = dict(zip(plan.wide, wide_in))

    right = (row, (col + 1) % n_col)
    left = (row, (col + n_col - 1) % n_col)
    first, last = n_col // 4, n_col // 4 * 3
    central = jnp.logical_and(col >= first, col < last)

    def col_peer(span, m):
        local = col % span
        return (row, col - local + (local + m) % span)

    def is_me(r, c):
        return jnp.logical_and(row == r, col == c)

    barrier = pltpu.get_barrier_semaphore()

    def greet(peer):
        pl.semaphore_signal(barrier, inc=1, device_id=peer, device_id_type=MESH)

    greet(left)
    greet(right)
    for level in plan.narrow:
        for m in range(1, 2**level):
            greet(col_peer(2**level, m))
    near = 2 + sum(2**level - 1 for level in plan.narrow)

    @pl.when(central)
    def _():
        for r in range(1, n_row):
            greet(((row + r) % n_row, col))
        for r in range(n_row):
            for c in range(1, n_col):
                greet(((row + r) % n_row, (col + c) % n_col))

    loads = [
        pltpu.make_async_copy(source, target, in_sem.at[i])
        for i, (source, target) in enumerate(
            ((cor_hbm, cor), (er_hbm, er), (sh_hbm, sh), (x_hbm, xt))
        )
    ]
    for load in loads:
        load.start()

    def assembled_rows(start, count):
        total = None
        for k in range(kinds):
            ids = cor[k : k + 1, :]
            at = lax.broadcasted_iota(jnp.int32, (count, elems), 0) + start
            onehot = jnp.where(at == ids, 1.0, 0.0).astype(BF16)
            term = jnp.dot(onehot, er[k], preferred_element_type=F32)
            total = term if total is None else total + term
        return total

    loads[0].wait()
    loads[1].wait()
    halo_out[...] = assembled_rows(rows_dev, 2 * shared).reshape(halo_out.shape)
    own[...] = assembled_rows(0, rows_dev)
    pl.semaphore_wait(barrier, near + n_row * n_col // 2 - central.astype(jnp.int32))

    def remote(source, target, send, recv, peer):
        return pltpu.make_async_remote_copy(
            src_ref=source,
            dst_ref=target,
            send_sem=send,
            recv_sem=recv,
            device_id=peer,
            device_id_type=MESH,
        )

    def sending(*args):
        copy = remote(*args)
        copy.start()
        return copy

    sent = []
    halo = [
        sending(halo_out.at[1], halo_in.at[0], halo_s.at[0], halo_r.at[0], right),
        sending(halo_out.at[0], halo_in.at[1], halo_s.at[1], halo_r.at[1], left),
    ]
    sent += halo

    loads[2].wait()
    targets = jnp.concatenate([sh[0:1, :], sh[1:2, :]], axis=1)
    at = lax.broadcasted_iota(jnp.int32, (rows_dev, 2 * shared), 0)
    share_map = jnp.where(at == targets, 1.0, 0.0).astype(BF16)
    share_map = jnp.concatenate([share_map, share_map], axis=1)
    loads[3].wait()
    turned[...] = xt[inner:, :].T
    for copy in halo:
        copy.wait_recv()
    received = halo_in[...].reshape(2 * shared, -1)
    high = received.astype(BF16)
    low = (received - high.astype(F32)).astype(BF16)
    received = jnp.concatenate([high, low], axis=0)
    assembled = own[...] + jnp.dot(share_map, received, preferred_element_type=F32)
    rhs[...] = assembled.astype(BF16)

    def partial(low, high):
        rows = xt[inner + sep * (low - 1) : inner + sep * high, :]
        block = jnp.dot(rows, rhs[...], preferred_element_type=F32)
        part[low - 1 : high] = block.reshape(high - low + 1, sep, -1)

    def place(level):
        span = plan.row_span(level)
        return row - row % span, row % span * n_col + col

    def owned(level):
        span, step = plan.row_span(level), plan.row_step(level)
        mine = jnp.logical_and(central, row % span % step == 0)
        index = row % span // step * (n_col // 2) + (col - first)
        rows = plan.piece(level)
        return mine, pl.ds(pl.multiple_of(jnp.where(mine, index, 0) * rows, 8), rows)

    def scatter(level):
        base, here = place(level)
        rows = plan.piece(level)
        for o, (r, c) in enumerate(plan.owners(level)):
            copy = remote(
                part.at[level - 1, pl.ds(o * rows, rows)],
                wide_in[level].at[here],
                wide_s.at[level - 1],
                wide_r.at[level - 1],
                (base + r, c),
            )

            @pl.when(jnp.logical_not(is_me(base + r, c)))
            def _():
                copy.start()

    def gather(level, some):
        base, _ = place(level)
        mine, rows = owned(level)
        block = final.at[level - 1, rows]

        @pl.when(mine)
        def _():
            for r, c in plan.members(level):
                if c in some:
                    copy = remote(block, block, ag_s.at[level - 1], ag_r.at[level - 1], (base + r, c))

                    @pl.when(jnp.logical_not(is_me(base + r, c)))
                    def _():
                        copy.start()

    def taken(buffer, sem):
        return pltpu.make_async_copy(buffer, buffer, sem)

    partial(plan.wide[-1], levels)
    for level in plan.wide:
        scatter(level)
    partial(1, plan.wide[-1] - 1)
    pair = sending(part.at[0], l1_in, l1_s.at[0], l1_r.at[0], col_peer(2, 1))
    sent.append(pair)

    def near_rows(level, ahead=0):
        span, rows = 2**level, sep // 2**level
        return pl.ds(pl.multiple_of((col % span + ahead) % span * rows, 8), rows)

    near_rs, near_ag = {}, {}
    for level in plan.narrow:
        for m in range(1, 2**level):
            near_rs[level, m] = sending(
                part.at[level - 1, near_rows(level, m)],
                near_in.at[level - 1, m - 1, pl.ds(0, sep // 2**level)],
                near_s.at[level - 1, m - 1],
                near_r.at[level - 1, m - 1],
                col_peer(2**level, m),
            )
    weights = jnp.dot(xt[:inner, :], rhs[...], preferred_element_type=F32).astype(BF16)
    out_ref[...] = tdot(xt[:inner, :], weights)

    early = range(2)
    for level in plan.wide:
        mine, rows = owned(level)
        _, here = place(level)
        count = wide_in[level].shape[0]

        @pl.when(mine)
        def _():
            wide_in[level][here] = part[level - 1, rows]
            taken(wide_in[level].at[pl.ds(0, count - 1)], wide_r.at[level - 1]).wait()
            total = wide_in[level][0]
            for k in range(1, count):
                total = total + wide_in[level][k]
            final[level - 1, rows] = total

        gather(level, early)
    for level in plan.narrow:
        rows = sep // 2**level
        total = part[level - 1, near_rows(level)]
        for m in range(1, 2**level):
            near_rs[level, m].wait_recv()
            total = total + near_in[level - 1, m - 1, pl.ds(0, rows)]
        final[level - 1, near_rows(level)] = total
        block = final.at[level - 1, near_rows(level)]
        for m in range(1, 2**level):
            near_ag[level, m] = sending(
                block, block, near_gs.at[level - 1, m - 1], near_gr.at[level - 1, m - 1], col_peer(2**level, m)
            )
    for level in plan.wide:
        gather(level, range(len(early), n_col))

    def applied(low, high):
        coef = final[low - 1 : high].reshape(sep * (high - low + 1), -1).astype(BF16)
        return jnp.dot(turned[:, sep * (low - 1) : sep * high], coef, preferred_element_type=F32)

    pair.wait_recv()
    final[0] = part[0] + l1_in[...]
    for copy in near_ag.values():
        copy.wait_recv()
    low = plan.wide[-1] - 1
    out_ref[...] += applied(1, low)

    for level in plan.wide:
        mine, _ = owned(level)
        others = sep - plan.piece(level)

        @pl.when(mine)
        def _():
            taken(final.at[level - 1, pl.ds(0, others)], ag_r.at[level - 1]).wait()

        @pl.when(jnp.logical_not(mine))
        def _():
            taken(final.at[level - 1], ag_r.at[level - 1]).wait()

    out_ref[...] += applied(low + 1, levels)
    sent += list(near_rs.values()) + list(near_ag.values())
    for copy in sent:
        copy.wait_send()
    for level in plan.wide:
        mine, _ = owned(level)
        others = sep - plan.piece(level)
        count = wide_in[level].shape[0]

        @pl.when(mine)
        def _():
            taken(part.at[level - 1, pl.ds(0, others)], wide_s.at[level - 1]).wait()
            taken(wide_in[level].at[pl.ds(0, count - 1)], ag_s.at[level - 1]).wait()

        @pl.when(jnp.logical_not(mine))
        def _():
            taken(part.at[level - 1], wide_s.at[level - 1]).wait()


def in_one_kernel(plan, elem_residual, corners, share_rows, x_factor):
    rows_dev, cols = x_factor.shape
    shared = share_rows.shape[2]
    elems, kinds, width = elem_residual.shape
    levels, sep = plan.levels, plan.sep
    slots = max(1, plan.n_col // 2 - 1)
    dma = pltpu.SemaphoreType.DMA
    anywhere = pl.BlockSpec(memory_space=pl.ANY)
    return pl.pallas_call(
        functools.partial(kernel, plan),
        out_shape=pltpu.VMEM((rows_dev, width), F32),
        in_specs=[anywhere] * 4,
        out_specs=pl.BlockSpec(memory_space=pltpu.VMEM),
        scratch_shapes=[
            pltpu.VMEM((kinds, elems, width), BF16),
            pltpu.VMEM((kinds, elems), jnp.int32),
            pltpu.VMEM((2, shared), jnp.int32),
            pltpu.VMEM((cols, rows_dev), BF16),
            pltpu.VMEM((2, shared, width), F32),
            pltpu.VMEM((2, shared, width), F32),
            pltpu.VMEM((rows_dev, width), F32),
            pltpu.VMEM((rows_dev, width), BF16),
            pltpu.VMEM((levels, sep, width), F32),
            pltpu.VMEM((sep, width), F32),
            pltpu.VMEM((levels, slots, sep // 4, width), F32),
            pltpu.VMEM((levels, sep, width), F32),
            pltpu.VMEM((rows_dev, sep * levels), BF16),
            dma((4,)),
            dma((2,)),
            dma((2,)),
            dma((1,)),
            dma((1,)),
            dma((levels, slots)),
            dma((levels, slots)),
            dma((levels, slots)),
            dma((levels, slots)),
            dma((levels,)),
            dma((levels,)),
            dma((levels,)),
            dma((levels,)),
        ]
        + [
            pltpu.VMEM((plan.row_span(level) * plan.n_col, plan.piece(level), width), F32)
            for level in plan.wide
        ],
        compiler_params=pltpu.CompilerParams(collective_id=0, has_side_effects=True),
        name="factor_solve",
    )(
        elem_residual.transpose(1, 0, 2),
        corners.T,
        share_rows.reshape(2, shared),
        x_factor.T,
    )


def solution(mesh):
    n_row, n_col = mesh.shape["row"], mesh.shape["col"]
    levels = (n_row * n_col).bit_length() - 1

    def per_device(elem_residual, corners, share_rows, x_factor):
        sep = (x_factor.shape[1] - INNER) // levels
        args = (elem_residual, corners, share_rows, x_factor)
        if takes(n_row, n_col, sep):
            return in_one_kernel(Plan(n_row, n_col, sep), *args)
        return by_rounds(n_row, n_col, *args)

    placed = (
        P(("row", "col"), None, None),
        P(("row", "col"), None),
        P(("row", "col"), None, None),
        P(("row", "col"), None),
    )
    return jax.shard_map(
        per_device, mesh=mesh, in_specs=placed, out_specs=P(("row", "col"), None), check_vma=False
    )
```

time: 25.7 us -> 25.1 us (0.977)
  Pallas kernels: 24.8 us -> 24.2 us
    pallas_call x1, Pallas kernels: 24.8 us -> 24.2 us  [in_one_kernel(): pl.pallas_call(functools.partial(kernel, plan), out_shape=pltpu.VMEM((row...]
where the time goes in v1:
time: 25.1 us; the launch traced here: 24.9 us
  Pallas kernels  24.2 us (96%)
  local copies, waits for them, and re-layouts  0.71 us (3%)
    pallas_call x1, Pallas kernels, in_one_kernel(): pl.pallas_call(functools.partial(kernel, plan), out_shape=pltpu.VMEM((row...  24.2 us
    unnamed x1, local copies, waits for them, and re-layouts  0.71 us

profile of v1, /device:TPU:0, one launch (start us, length us, event | category | flops | bytes accessed | tf_op | source)
XLA Modules:
  0.0 24.9 jit_solution(187492362384055706)
XLA Ops:
  0.0 24.2 %factor_solve.1 = f32[256,256]{1,0:T(8,128)S(1)} custom-call(bf16[3,512,256]{2,1,0:T(8,128)(2,1)} %bitcast.5, s32[3,512]{1,0:T(4,128)} %bitcast.6, s32[2,64]{1,0:T(2,128)} %bitcast.7, bf16[1728,256]{1,0:T(8,128)(2,1)} %bitcast.4), custom_call_target="tpu_custom_call" | custom-call | tf_op jit(solution)/shard_map/factor_solve/pallas_call | solution.py:372
  24.2 0.7 %copy.6 = f32[256,256]{1,0:T(8,128)} copy(f32[256,256]{1,0:T(8,128)S(1)} %factor_solve.1) | data formatting | bytes 524288

commit v2 on v1

--- a/solution.py
+++ b/solution.py
@@ -69,24 +69,21 @@
         self.n_row, self.n_col, self.sep = n_row, n_col, sep
         self.levels = (n_row * n_col).bit_length() - 1
         self.col_bits = n_col.bit_length() - 1
-        self.wide = list(range(self.levels, self.col_bits - 1, -1))
+        self.wide = list(range(self.col_bits, self.levels + 1))
+        self.upper = self.wide[1:]
         self.narrow = list(range(self.col_bits - 1, 1, -1))
 
     def row_span(self, level):
         return max(1, 2**level // self.n_col)
 
-    def row_step(self, level):
-        return self.n_col // 2 * self.row_span(level) // self.n_owners(level)
-
-    def n_owners(self, level):
-        return min(self.n_col // 2 * self.row_span(level), self.sep // 8)
+    def halves(self, level):
+        return 2 if self.row_span(level) > 1 else 1
 
     def piece(self, level):
-        return self.sep // self.n_owners(level)
-
-    def owners(self, level):
-        rows = range(0, self.row_span(level), self.row_step(level))
-        return [(r, self.n_col // 4 + c) for r in rows for c in range(self.n_col // 2)]
+        return self.sep // (self.n_col // 2 * self.halves(level))
+
+    def sources(self, level):
+        return self.row_span(level) // self.halves(level) * self.n_col
 
     def members(self, level):
         every = [(r, c) for r in range(self.row_span(level)) for c in range(self.n_col)]
@@ -106,8 +103,8 @@
     er_hbm, cor_hbm, sh_hbm, x_hbm,
     out_ref,
     er, cor, sh, xt,
-    halo_out, halo_in, own, rhs, part, l1_in, near_in, final, turned,
-    in_sem, halo_s, halo_r, l1_s, l1_r, near_s, near_r, near_gs, near_gr, wide_s, wide_r, ag_s, ag_r,
+    halo_out, halo_in, own, rhs, part, l1_in, pair_in, near_in, final, turned,
+    in_sem, halo_s, halo_r, pair_s, pair_r, l1_s, l1_r, near_s, near_r, near_gs, near_gr, wide_s, wide_r, ag_s, ag_r,
     *wide_in,
 ):
     row, col = lax.axis_index("row"), lax.axis_index("col")
@@ -138,10 +135,11 @@
 
     greet(left)
     greet(right)
+    greet((row ^ 1, col))
     for level in plan.narrow:
         for m in range(1, 2**level):
             greet(col_peer(2**level, m))
-    near = 2 + sum(2**level - 1 for level in plan.narrow)
+    near = 3 + sum(2**level - 1 for level in plan.narrow)
 
     @pl.when(central)
     def _():
@@ -219,36 +217,37 @@
         block = jnp.dot(rows, rhs[...], preferred_element_type=F32)
         part[low - 1 : high] = block.reshape(high - low + 1, sep, -1)
 
-    def place(level):
-        span = plan.row_span(level)
-        return row - row % span, row % span * n_col + col
+    half = row % 2
 
     def owned(level):
-        span, step = plan.row_span(level), plan.row_step(level)
-        mine = jnp.logical_and(central, row % span % step == 0)
-        index = row % span // step * (n_col // 2) + (col - first)
+        span, halves = plan.row_span(level), plan.halves(level)
+        base = row - row % span
+        mine = jnp.logical_and(central, row == base + half * (span - 1))
+        index = half * (halves - 1) * (n_col // 2) + (col - first)
         rows = plan.piece(level)
-        return mine, pl.ds(pl.multiple_of(jnp.where(mine, index, 0) * rows, 8), rows)
+        slot = row % span // halves * n_col + col
+        return mine, pl.ds(pl.multiple_of(jnp.where(mine, index, 0) * rows, 8), rows), slot, base
 
     def scatter(level):
-        base, here = place(level)
-        rows = plan.piece(level)
-        for o, (r, c) in enumerate(plan.owners(level)):
+        _, _, slot, base = owned(level)
+        rows, halves = plan.piece(level), plan.halves(level)
+        start = half * (halves - 1) * (sep // 2)
+        target = base + half * (plan.row_span(level) - 1)
+        for c in range(n_col // 2):
             copy = remote(
-                part.at[level - 1, pl.ds(o * rows, rows)],
-                wide_in[level].at[here],
+                part.at[level - 1, pl.ds(pl.multiple_of(start + c * rows, 8), rows)],
+                wide_in[level].at[slot],
                 wide_s.at[level - 1],
                 wide_r.at[level - 1],
-                (base + r, c),
+                (target, first + c),
             )
 
-            @pl.when(jnp.logical_not(is_me(base + r, c)))
+            @pl.when(jnp.logical_not(is_me(target, first + c)))
             def _():
                 copy.start()
 
     def gather(level, some):
-        base, _ = place(level)
-        mine, rows = owned(level)
+        mine, rows, _, base = owned(level)
         block = final.at[level - 1, rows]
 
         @pl.when(mine)
@@ -264,10 +263,19 @@
     def taken(buffer, sem):
         return pltpu.make_async_copy(buffer, buffer, sem)
 
-    partial(plan.wide[-1], levels)
-    for level in plan.wide:
+    partial(plan.wide[0], levels)
+    kept = pl.ds(pl.multiple_of(half * (sep // 2), 8), sep // 2)
+    given = pl.ds(pl.multiple_of((1 - half) * (sep // 2), 8), sep // 2)
+    over = pl.ds(plan.upper[0] - 1, len(plan.upper))
+    cores = sending(part.at[over, given], pair_in, pair_s.at[0], pair_r.at[0], (row ^ 1, col))
+    sent.append(cores)
+    scatter(plan.wide[0])
+    cores.wait_recv()
+    for i, level in enumerate(plan.upper):
+        part[level - 1, kept] += pair_in[i]
+    for level in reversed(plan.upper):
         scatter(level)
-    partial(1, plan.wide[-1] - 1)
+    partial(1, plan.wide[0] - 1)
     pair = sending(part.at[0], l1_in, l1_s.at[0], l1_r.at[0], col_peer(2, 1))
     sent.append(pair)
 
@@ -289,14 +297,13 @@
     out_ref[...] = tdot(xt[:inner, :], weights)
 
     early = range(2)
-    for level in plan.wide:
-        mine, rows = owned(level)
-        _, here = place(level)
-        count = wide_in[level].shape[0]
+    for level in plan.wide[:1] + plan.upper[::-1]:
+        mine, rows, slot, _ = owned(level)
+        count = plan.sources(level)
 
         @pl.when(mine)
         def _():
-            wide_in[level][here] = part[level - 1, rows]
+            wide_in[level][slot] = part[level - 1, rows]
             taken(wide_in[level].at[pl.ds(0, count - 1)], wide_r.at[level - 1]).wait()
             total = wide_in[level][0]
             for k in range(1, count):
@@ -327,11 +334,11 @@
     final[0] = part[0] + l1_in[...]
     for copy in near_ag.values():
         copy.wait_recv()
-    low = plan.wide[-1] - 1
+    low = plan.wide[0] - 1
     out_ref[...] += applied(1, low)
 
     for level in plan.wide:
-        mine, _ = owned(level)
+        mine = owned(level)[0]
         others = sep - plan.piece(level)
 
         @pl.when(mine)
@@ -347,18 +354,19 @@
     for copy in sent:
         copy.wait_send()
     for level in plan.wide:
-        mine, _ = owned(level)
-        others = sep - plan.piece(level)
-        count = wide_in[level].shape[0]
+        mine = owned(level)[0]
+        mass = sep // plan.halves(level)
+        rows = plan.piece(level)
+        members = plan.row_span(level) * n_col
 
         @pl.when(mine)
         def _():
-            taken(part.at[level - 1, pl.ds(0, others)], wide_s.at[level - 1]).wait()
-            taken(wide_in[level].at[pl.ds(0, count - 1)], ag_s.at[level - 1]).wait()
+            taken(part.at[level - 1, pl.ds(0, mass - rows)], wide_s.at[level - 1]).wait()
+            taken(wide_in[level].at[pl.ds(0, members - 1)], ag_s.at[level - 1]).wait()
 
         @pl.when(jnp.logical_not(mine))
         def _():
-            taken(part.at[level - 1], wide_s.at[level - 1]).wait()
+            taken(part.at[level - 1, pl.ds(0, mass)], wide_s.at[level - 1]).wait()
 
 
 def in_one_kernel(plan, elem_residual, corners, share_rows, x_factor):
@@ -385,12 +393,15 @@
             pltpu.VMEM((rows_dev, width), BF16),
             pltpu.VMEM((levels, sep, width), F32),
             pltpu.VMEM((sep, width), F32),
+            pltpu.VMEM((len(plan.upper), sep // 2, width), F32),
             pltpu.VMEM((levels, slots, sep // 4, width), F32),
             pltpu.VMEM((levels, sep, width), F32),
             pltpu.VMEM((rows_dev, sep * levels), BF16),
             dma((4,)),
             dma((2,)),
             dma((2,)),
+            dma((1,)),
+            dma((1,)),
             dma((1,)),
             dma((1,)),
             dma((levels, slots)),

time: 25.1 us -> 24.2 us (0.964)
  Pallas kernels: 24.2 us -> 23.3 us
    pallas_call x1, Pallas kernels: 24.2 us -> 23.3 us  [in_one_kernel(): pl.pallas_call(functools.partial(kernel, plan), out_shape=pltpu.VMEM((row...]
where the time goes in v2:
time: 24.2 us; the launch traced here: 24 us
  Pallas kernels  23.3 us (96%)
  local copies, waits for them, and re-layouts  0.71 us (3%)
    pallas_call x1, Pallas kernels, in_one_kernel(): pl.pallas_call(functools.partial(kernel, plan), out_shape=pltpu.VMEM((row...  23.3 us
    unnamed x1, local copies, waits for them, and re-layouts  0.71 us

profile of v2, /device:TPU:0, one launch (start us, length us, event | category | flops | bytes accessed | tf_op | source)
XLA Modules:
  0.0 24.0 jit_solution(8782631674498305888)
XLA Ops:
  0.0 23.3 %factor_solve.1 = f32[256,256]{1,0:T(8,128)S(1)} custom-call(bf16[3,512,256]{2,1,0:T(8,128)(2,1)} %bitcast.5, s32[3,512]{1,0:T(4,128)} %bitcast.6, s32[2,64]{1,0:T(2,128)} %bitcast.7, bf16[1728,256]{1,0:T(8,128)(2,1)} %bitcast.4), custom_call_target="tpu_custom_call" | custom-call | tf_op jit(solution)/shard_map/factor_solve/pallas_call | solution.py:380
  23.3 0.7 %copy.6 = f32[256,256]{1,0:T(8,128)} copy(f32[256,256]{1,0:T(8,128)S(1)} %factor_solve.1) | data formatting | bytes 524288

commit v3 on v2

--- a/solution.py
+++ b/solution.py
@@ -8,6 +8,7 @@
 from jax.sharding import PartitionSpec as P
 
 INNER = 1408
+OUTER = (0, 2, 3, 1)
 MESH = pl.DeviceIdType.MESH
 F32 = jnp.float32
 BF16 = jnp.bfloat16
@@ -87,7 +88,8 @@
 
     def members(self, level):
         every = [(r, c) for r in range(self.row_span(level)) for c in range(self.n_col)]
-        return sorted(every, key=lambda at: (at[1] // 2, at[0] % 2, at[1], at[0]))
+        every = [at for at in every if at[0] % self.halves(level) == 0]
+        return sorted(every, key=lambda at: (OUTER[at[1] * 4 // self.n_col], at[0] % 2, at[1], at[0]))
 
 
 def takes(n_row, n_col, sep):
@@ -103,8 +105,8 @@
     er_hbm, cor_hbm, sh_hbm, x_hbm,
     out_ref,
     er, cor, sh, xt,
-    halo_out, halo_in, own, rhs, part, l1_in, pair_in, near_in, final, turned,
-    in_sem, halo_s, halo_r, pair_s, pair_r, l1_s, l1_r, near_s, near_r, near_gs, near_gr, wide_s, wide_r, ag_s, ag_r,
+    halo_out, halo_in, own, rhs, part, l1_in, pair_in, near_in, final, turned, shared_rows, passed_in,
+    in_sem, halo_s, halo_r, pair_s, pair_r, passed_s, passed_r, l1_s, l1_r, near_s, near_r, near_gs, near_gr, wide_s, wide_r, ag_s, ag_r,
     *wide_in,
 ):
     row, col = lax.axis_index("row"), lax.axis_index("col")
@@ -113,7 +115,6 @@
     shared = halo_out.shape[1]
     kinds = er.shape[0]
     elems = er.shape[1]
-    inner = xt.shape[0] - sep * levels
     wide_in = dict(zip(plan.wide, wide_in))
 
     right = (row, (col + 1) % n_col)
@@ -149,18 +150,23 @@
             for c in range(1, n_col):
                 greet(((row + r) % n_row, (col + c) % n_col))
 
+    inner = xt.shape[0] - sep * levels
+    low = plan.wide[0] - 1
+    wide_at = inner + sep * low
+    parts = [(cor_hbm, cor)]
+    parts += [(er_hbm.at[k], er.at[k]) for k in range(kinds)]
+    parts += [(sh_hbm, sh), (x_hbm.at[wide_at:], xt.at[wide_at:]), (x_hbm.at[:wide_at], xt.at[:wide_at])]
     loads = [
-        pltpu.make_async_copy(source, target, in_sem.at[i])
-        for i, (source, target) in enumerate(
-            ((cor_hbm, cor), (er_hbm, er), (sh_hbm, sh), (x_hbm, xt))
-        )
+        pltpu.make_async_copy(source, target, in_sem.at[i]) for i, (source, target) in enumerate(parts)
     ]
-    for load in loads:
+    for load in loads[: kinds + 1]:
         load.start()
 
-    def assembled_rows(start, count):
+    def assembled_rows(start, count, start_done=True):
         total = None
         for k in range(kinds):
+            if not start_done:
+                loads[k + 1].wait()
             ids = cor[k : k + 1, :]
             at = lax.broadcasted_iota(jnp.int32, (count, elems), 0) + start
             onehot = jnp.where(at == ids, 1.0, 0.0).astype(BF16)
@@ -169,10 +175,13 @@
         return total
 
     loads[0].wait()
-    loads[1].wait()
-    halo_out[...] = assembled_rows(rows_dev, 2 * shared).reshape(halo_out.shape)
-    own[...] = assembled_rows(0, rows_dev)
+    halo_out[...] = assembled_rows(rows_dev, 2 * shared, False).reshape(halo_out.shape)
+    for load in loads[kinds + 1 :]:
+        load.start()
     pl.semaphore_wait(barrier, near + n_row * n_col // 2 - central.astype(jnp.int32))
+
+    def taken(buffer, sem):
+        return pltpu.make_async_copy(buffer, buffer, sem)
 
     def remote(source, target, send, recv, peer):
         return pltpu.make_async_remote_copy(
@@ -190,32 +199,39 @@
         return copy
 
     sent = []
+    away = col % 2
+    near_side = 1 - away
+    far_peer = (row, (col + n_col - 1 + 2 * away) % n_col)
+    near_peer = (row, (col + n_col - 1 + 2 * near_side) % n_col)
     halo = [
-        sending(halo_out.at[1], halo_in.at[0], halo_s.at[0], halo_r.at[0], right),
-        sending(halo_out.at[0], halo_in.at[1], halo_s.at[1], halo_r.at[1], left),
+        sending(halo_out.at[away], halo_in.at[near_side], halo_s.at[0], halo_r.at[near_side], far_peer),
+        sending(halo_out.at[near_side], halo_in.at[away], halo_s.at[1], halo_r.at[away], near_peer),
     ]
     sent += halo
 
-    loads[2].wait()
+    def split(value):
+        high = value.astype(BF16)
+        return high, (value - high.astype(F32)).astype(BF16)
+
+    own[...] = assembled_rows(0, rows_dev)
+    loads[kinds + 1].wait()
     targets = jnp.concatenate([sh[0:1, :], sh[1:2, :]], axis=1)
     at = lax.broadcasted_iota(jnp.int32, (rows_dev, 2 * shared), 0)
     share_map = jnp.where(at == targets, 1.0, 0.0).astype(BF16)
     share_map = jnp.concatenate([share_map, share_map], axis=1)
-    loads[3].wait()
+    loads[kinds + 2].wait()
+    rows = xt[wide_at:, :]
+    high, fine = split(own[...])
+    of_own = jnp.dot(rows, high, preferred_element_type=F32) + jnp.dot(rows, fine, preferred_element_type=F32)
+    part[low:] = of_own.reshape(len(plan.wide), sep, -1)
+    shared_rows[...] = jnp.dot(rows, share_map, preferred_element_type=F32).astype(BF16)
+    loads[kinds + 3].wait()
     turned[...] = xt[inner:, :].T
-    for copy in halo:
-        copy.wait_recv()
-    received = halo_in[...].reshape(2 * shared, -1)
-    high = received.astype(BF16)
-    low = (received - high.astype(F32)).astype(BF16)
-    received = jnp.concatenate([high, low], axis=0)
-    assembled = own[...] + jnp.dot(share_map, received, preferred_element_type=F32)
-    rhs[...] = assembled.astype(BF16)
-
-    def partial(low, high):
-        rows = xt[inner + sep * (low - 1) : inner + sep * high, :]
-        block = jnp.dot(rows, rhs[...], preferred_element_type=F32)
-        part[low - 1 : high] = block.reshape(high - low + 1, sep, -1)
+    for side in range(2):
+        taken(halo_in.at[side], halo_r.at[side]).wait()
+    received = jnp.concatenate(split(halo_in[...].reshape(2 * shared, -1)), axis=0)
+    block = jnp.dot(shared_rows[...], received, preferred_element_type=F32)
+    part[low:] += block.reshape(len(plan.wide), sep, -1)
 
     half = row % 2
 
@@ -260,10 +276,6 @@
                     def _():
                         copy.start()
 
-    def taken(buffer, sem):
-        return pltpu.make_async_copy(buffer, buffer, sem)
-
-    partial(plan.wide[0], levels)
     kept = pl.ds(pl.multiple_of(half * (sep // 2), 8), sep // 2)
     given = pl.ds(pl.multiple_of((1 - half) * (sep // 2), 8), sep // 2)
     over = pl.ds(plan.upper[0] - 1, len(plan.upper))
@@ -275,7 +287,10 @@
         part[level - 1, kept] += pair_in[i]
     for level in reversed(plan.upper):
         scatter(level)
-    partial(1, plan.wide[0] - 1)
+    assembled = own[...] + jnp.dot(share_map, received, preferred_element_type=F32)
+    rhs[...] = assembled.astype(BF16)
+    block = jnp.dot(xt[inner:wide_at, :], rhs[...], preferred_element_type=F32)
+    part[:low] = block.reshape(low, sep, -1)
     pair = sending(part.at[0], l1_in, l1_s.at[0], l1_r.at[0], col_peer(2, 1))
     sent.append(pair)
 
@@ -296,7 +311,7 @@
     weights = jnp.dot(xt[:inner, :], rhs[...], preferred_element_type=F32).astype(BF16)
     out_ref[...] = tdot(xt[:inner, :], weights)
 
-    early = range(2)
+    outer = [c for c in range(n_col) if OUTER[c * 4 // n_col] < 2]
     for level in plan.wide[:1] + plan.upper[::-1]:
         mine, rows, slot, _ = owned(level)
         count = plan.sources(level)
@@ -310,7 +325,7 @@
                 total = total + wide_in[level][k]
             final[level - 1, rows] = total
 
-        gather(level, early)
+        gather(level, outer)
     for level in plan.narrow:
         rows = sep // 2**level
         total = part[level - 1, near_rows(level)]
@@ -324,7 +339,7 @@
                 block, block, near_gs.at[level - 1, m - 1], near_gr.at[level - 1, m - 1], col_peer(2**level, m)
             )
     for level in plan.wide:
-        gather(level, range(len(early), n_col))
+        gather(level, [c for c in range(n_col) if c not in outer])
 
     def applied(low, high):
         coef = final[low - 1 : high].reshape(sep * (high - low + 1), -1).astype(BF16)
@@ -334,10 +349,15 @@
     final[0] = part[0] + l1_in[...]
     for copy in near_ag.values():
         copy.wait_recv()
-    low = plan.wide[0] - 1
     out_ref[...] += applied(1, low)
 
-    for level in plan.wide:
+    even = half == 0
+    passed = [
+        remote(final.at[level - 1], passed_in.at[i], passed_s.at[i], passed_r.at[i], (row ^ 1, col))
+        for i, level in enumerate(plan.upper)
+    ]
+
+    def arrived(level):
         mine = owned(level)[0]
         others = sep - plan.piece(level)
 
@@ -349,7 +369,27 @@
         def _():
             taken(final.at[level - 1], ag_r.at[level - 1]).wait()
 
-    out_ref[...] += applied(low + 1, levels)
+    @pl.when(even)
+    def _():
+        for level in reversed(plan.upper):
+            arrived(level)
+            passed[plan.upper.index(level)].start()
+
+    arrived(plan.wide[0])
+
+    @pl.when(even)
+    def _():
+        out_ref[...] += applied(low + 1, levels)
+        for copy in passed:
+            copy.wait_send()
+
+    @pl.when(jnp.logical_not(even))
+    def _():
+        for copy in passed:
+            copy.wait_recv()
+        coef = jnp.concatenate([final[low], passed_in[...].reshape(len(plan.upper) * sep, -1)], axis=0)
+        out_ref[...] += jnp.dot(turned[:, sep * low :], coef.astype(BF16), preferred_element_type=F32)
+
     sent += list(near_rs.values()) + list(near_ag.values())
     for copy in sent:
         copy.wait_send()
@@ -362,11 +402,22 @@
         @pl.when(mine)
         def _():
             taken(part.at[level - 1, pl.ds(0, mass - rows)], wide_s.at[level - 1]).wait()
-            taken(wide_in[level].at[pl.ds(0, members - 1)], ag_s.at[level - 1]).wait()
+            if plan.halves(level) == 1:
+                taken(wide_in[level].at[pl.ds(0, members - 1)], ag_s.at[level - 1]).wait()
 
         @pl.when(jnp.logical_not(mine))
         def _():
             taken(part.at[level - 1, pl.ds(0, mass)], wide_s.at[level - 1]).wait()
+
+        if plan.halves(level) == 2:
+
+            @pl.when(jnp.logical_and(mine, even))
+            def _():
+                taken(wide_in[level].at[pl.ds(0, members // 2 - 1)], ag_s.at[level - 1]).wait()
+
+            @pl.when(jnp.logical_and(mine, jnp.logical_not(even)))
+            def _():
+                taken(wide_in[level].at[pl.ds(0, members // 2)], ag_s.at[level - 1]).wait()
 
 
 def in_one_kernel(plan, elem_residual, corners, share_rows, x_factor):
@@ -397,11 +448,15 @@
             pltpu.VMEM((levels, slots, sep // 4, width), F32),
             pltpu.VMEM((levels, sep, width), F32),
             pltpu.VMEM((rows_dev, sep * levels), BF16),
-            dma((4,)),
+            pltpu.VMEM((len(plan.wide) * sep, 4 * shared), BF16),
+            pltpu.VMEM((len(plan.upper), sep, width), F32),
+            dma((kinds + 4,)),
             dma((2,)),
             dma((2,)),
             dma((1,)),
             dma((1,)),
+            dma((len(plan.upper),)),
+            dma((len(plan.upper),)),
             dma((1,)),
             dma((1,)),
             dma((levels, slots)),

time: 24.2 us -> 23.7 us (0.979)
  Pallas kernels: 23.3 us -> 22.8 us
    pallas_call x1, Pallas kernels: 23.3 us -> 22.8 us  [in_one_kernel(): pl.pallas_call(functools.partial(kernel, plan), out_shape=pltpu.VMEM((row...]
where the time goes in v3:
time: 23.7 us; the launch traced here: 23.5 us
  Pallas kernels  22.8 us (96%)
  local copies, waits for them, and re-layouts  0.71 us (3%)
    pallas_call x1, Pallas kernels, in_one_kernel(): pl.pallas_call(functools.partial(kernel, plan), out_shape=pltpu.VMEM((row...  22.8 us
    unnamed x1, local copies, waits for them, and re-layouts  0.71 us

profile of v3, /device:TPU:0, one launch (start us, length us, event | category | flops | bytes accessed | tf_op | source)
XLA Modules:
  0.0 23.5 jit_solution(15205594999243320449)
XLA Ops:
  0.0 22.8 %factor_solve.1 = f32[256,256]{1,0:T(8,128)S(1)} custom-call(bf16[3,512,256]{2,1,0:T(8,128)(2,1)} %bitcast.5, s32[3,512]{1,0:T(4,128)} %bitcast.6, s32[2,64]{1,0:T(2,128)} %bitcast.7, bf16[1728,256]{1,0:T(8,128)(2,1)} %bitcast.4), custom_call_target="tpu_custom_call" | custom-call | tf_op jit(solution)/shard_map/factor_solve/pallas_call | solution.py:431
  22.8 0.7 %copy.6 = f32[256,256]{1,0:T(8,128)} copy(f32[256,256]{1,0:T(8,128)S(1)} %factor_solve.1) | data formatting | bytes 524288

commit v4 on v3

--- a/solution.py
+++ b/solution.py
@@ -249,7 +249,8 @@
         rows, halves = plan.piece(level), plan.halves(level)
         start = half * (halves - 1) * (sep // 2)
         target = base + half * (plan.row_span(level) - 1)
-        for c in range(n_col // 2):
+        for k in range(n_col // 2):
+            c = jnp.where(col < n_col // 2, n_col // 2 - 1 - k, k)
             copy = remote(
                 part.at[level - 1, pl.ds(pl.multiple_of(start + c * rows, 8), rows)],
                 wide_in[level].at[slot],
@@ -282,17 +283,10 @@
     cores = sending(part.at[over, given], pair_in, pair_s.at[0], pair_r.at[0], (row ^ 1, col))
     sent.append(cores)
     scatter(plan.wide[0])
-    cores.wait_recv()
-    for i, level in enumerate(plan.upper):
-        part[level - 1, kept] += pair_in[i]
-    for level in reversed(plan.upper):
-        scatter(level)
     assembled = own[...] + jnp.dot(share_map, received, preferred_element_type=F32)
     rhs[...] = assembled.astype(BF16)
     block = jnp.dot(xt[inner:wide_at, :], rhs[...], preferred_element_type=F32)
     part[:low] = block.reshape(low, sep, -1)
-    pair = sending(part.at[0], l1_in, l1_s.at[0], l1_r.at[0], col_peer(2, 1))
-    sent.append(pair)
 
     def near_rows(level, ahead=0):
         span, rows = 2**level, sep // 2**level
@@ -308,8 +302,29 @@
                 near_r.at[level - 1, m - 1],
                 col_peer(2**level, m),
             )
+    cores.wait_recv()
+    for i, level in enumerate(plan.upper):
+        part[level - 1, kept] += pair_in[i]
+    for level in reversed(plan.upper):
+        scatter(level)
     weights = jnp.dot(xt[:inner, :], rhs[...], preferred_element_type=F32).astype(BF16)
     out_ref[...] = tdot(xt[:inner, :], weights)
+
+    pair = sending(part.at[0], l1_in, l1_s.at[0], l1_r.at[0], col_peer(2, 1))
+    sent.append(pair)
+    def gather_near():
+        for level in plan.narrow:
+            rows = sep // 2**level
+            total = part[level - 1, near_rows(level)]
+            for m in range(1, 2**level):
+                near_rs[level, m].wait_recv()
+                total = total + near_in[level - 1, m - 1, pl.ds(0, rows)]
+            final[level - 1, near_rows(level)] = total
+            block = final.at[level - 1, near_rows(level)]
+            for m in range(1, 2**level):
+                near_ag[level, m] = sending(
+                    block, block, near_gs.at[level - 1, m - 1], near_gr.at[level - 1, m - 1], col_peer(2**level, m)
+                )
 
     outer = [c for c in range(n_col) if OUTER[c * 4 // n_col] < 2]
     for level in plan.wide[:1] + plan.upper[::-1]:
@@ -326,18 +341,8 @@
             final[level - 1, rows] = total
 
         gather(level, outer)
-    for level in plan.narrow:
-        rows = sep // 2**level
-        total = part[level - 1, near_rows(level)]
-        for m in range(1, 2**level):
-            near_rs[level, m].wait_recv()
-            total = total + near_in[level - 1, m - 1, pl.ds(0, rows)]
-        final[level - 1, near_rows(level)] = total
-        block = final.at[level - 1, near_rows(level)]
-        for m in range(1, 2**level):
-            near_ag[level, m] = sending(
-                block, block, near_gs.at[level - 1, m - 1], near_gr.at[level - 1, m - 1], col_peer(2**level, m)
-            )
+        if level == plan.wide[0]:
+            gather_near()
     for level in plan.wide:
         gather(level, [c for c in range(n_col) if c not in outer])
 

time: 23.7 us -> 23.4 us (0.987)
  Pallas kernels: 22.8 us -> 22.5 us
    pallas_call x1, Pallas kernels: 22.8 us -> 22.5 us  [in_one_kernel(): pl.pallas_call(functools.partial(kernel, plan), out_shape=pltpu.VMEM((row...]
where the time goes in v4:
time: 23.4 us; the launch traced here: 23.2 us
  Pallas kernels  22.5 us (96%)
  local copies, waits for them, and re-layouts  0.71 us (3%)
    pallas_call x1, Pallas kernels, in_one_kernel(): pl.pallas_call(functools.partial(kernel, plan), out_shape=pltpu.VMEM((row...  22.5 us
    unnamed x1, local copies, waits for them, and re-layouts  0.71 us

profile of v4, /device:TPU:0, one launch (start us, length us, event | category | flops | bytes accessed | tf_op | source)
XLA Modules:
  0.0 23.2 jit_solution(3082903892354717662)
XLA Ops:
  0.0 22.5 %factor_solve.1 = f32[256,256]{1,0:T(8,128)S(1)} custom-call(bf16[3,512,256]{2,1,0:T(8,128)(2,1)} %bitcast.5, s32[3,512]{1,0:T(4,128)} %bitcast.6, s32[2,64]{1,0:T(2,128)} %bitcast.7, bf16[1728,256]{1,0:T(8,128)(2,1)} %bitcast.4), custom_call_target="tpu_custom_call" | custom-call | tf_op jit(solution)/shard_map/factor_solve/pallas_call | solution.py:436
  22.5 0.7 %copy.6 = f32[256,256]{1,0:T(8,128)} copy(f32[256,256]{1,0:T(8,128)S(1)} %factor_solve.1) | data formatting | bytes 524288

commit v5 on v4

--- a/solution.py
+++ b/solution.py
@@ -204,8 +204,8 @@
     far_peer = (row, (col + n_col - 1 + 2 * away) % n_col)
     near_peer = (row, (col + n_col - 1 + 2 * near_side) % n_col)
     halo = [
+        sending(halo_out.at[near_side], halo_in.at[away], halo_s.at[1], halo_r.at[away], near_peer),
         sending(halo_out.at[away], halo_in.at[near_side], halo_s.at[0], halo_r.at[near_side], far_peer),
-        sending(halo_out.at[near_side], halo_in.at[away], halo_s.at[1], halo_r.at[away], near_peer),
     ]
     sent += halo
 

time: 23.4 us -> 23.4 us (level)
  no operation moved by 1% of the time
where the time goes in v5:
time: 23.4 us; the launch traced here: 23.2 us
  Pallas kernels  22.5 us (96%)
  local copies, waits for them, and re-layouts  0.71 us (3%)
    pallas_call x1, Pallas kernels, in_one_kernel(): pl.pallas_call(functools.partial(kernel, plan), out_shape=pltpu.VMEM((row...  22.5 us
    unnamed x1, local copies, waits for them, and re-layouts  0.71 us

profile of v5, /device:TPU:0, one launch (start us, length us, event | category | flops | bytes accessed | tf_op | source)
XLA Modules:
  0.0 23.2 jit_solution(13424932914416748501)
XLA Ops:
  0.0 22.5 %factor_solve.1 = f32[256,256]{1,0:T(8,128)S(1)} custom-call(bf16[3,512,256]{2,1,0:T(8,128)(2,1)} %bitcast.5, s32[3,512]{1,0:T(4,128)} %bitcast.6, s32[2,64]{1,0:T(2,128)} %bitcast.7, bf16[1728,256]{1,0:T(8,128)(2,1)} %bitcast.4), custom_call_target="tpu_custom_call" | custom-call | tf_op jit(solution)/shard_map/factor_solve/pallas_call | solution.py:436
  22.5 0.7 %copy.6 = f32[256,256]{1,0:T(8,128)} copy(f32[256,256]{1,0:T(8,128)S(1)} %factor_solve.1) | data formatting | bytes 524288

commit v6 on v4

--- a/solution.py
+++ b/solution.py
@@ -279,9 +279,13 @@
 
     kept = pl.ds(pl.multiple_of(half * (sep // 2), 8), sep // 2)
     given = pl.ds(pl.multiple_of((1 - half) * (sep // 2), 8), sep // 2)
-    over = pl.ds(plan.upper[0] - 1, len(plan.upper))
-    cores = sending(part.at[over, given], pair_in, pair_s.at[0], pair_r.at[0], (row ^ 1, col))
-    sent.append(cores)
+    cores = {
+        level: sending(
+            part.at[level - 1, given], pair_in.at[i], pair_s.at[i], pair_r.at[i], (row ^ 1, col)
+        )
+        for i, level in reversed(list(enumerate(plan.upper)))
+    }
+    sent += list(cores.values())
     scatter(plan.wide[0])
     assembled = own[...] + jnp.dot(share_map, received, preferred_element_type=F32)
     rhs[...] = assembled.astype(BF16)
@@ -302,10 +306,9 @@
                 near_r.at[level - 1, m - 1],
                 col_peer(2**level, m),
             )
-    cores.wait_recv()
-    for i, level in enumerate(plan.upper):
+    for i, level in reversed(list(enumerate(plan.upper))):
+        cores[level].wait_recv()
         part[level - 1, kept] += pair_in[i]
-    for level in reversed(plan.upper):
         scatter(level)
     weights = jnp.dot(xt[:inner, :], rhs[...], preferred_element_type=F32).astype(BF16)
     out_ref[...] = tdot(xt[:inner, :], weights)
@@ -458,8 +461,8 @@
             dma((kinds + 4,)),
             dma((2,)),
             dma((2,)),
-            dma((1,)),
-            dma((1,)),
+            dma((len(plan.upper),)),
+            dma((len(plan.upper),)),
             dma((len(plan.upper),)),
             dma((len(plan.upper),)),
             dma((1,)),

time: 23.4 us -> 23.5 us (level)
  no operation moved by 1% of the time
where the time goes in v6:
time: 23.5 us; the launch traced here: 23.2 us
  Pallas kernels  22.5 us (96%)
  local copies, waits for them, and re-layouts  0.71 us (3%)
    pallas_call x1, Pallas kernels, in_one_kernel(): pl.pallas_call(functools.partial(kernel, plan), out_shape=pltpu.VMEM((row...  22.5 us
    unnamed x1, local copies, waits for them, and re-layouts  0.71 us

profile of v6, /device:TPU:0, one launch (start us, length us, event | category | flops | bytes accessed | tf_op | source)
XLA Modules:
  0.0 23.2 jit_solution(7145578341016857706)
XLA Ops:
  0.0 22.5 %factor_solve.1 = f32[256,256]{1,0:T(8,128)S(1)} custom-call(bf16[3,512,256]{2,1,0:T(8,128)(2,1)} %bitcast.5, s32[3,512]{1,0:T(4,128)} %bitcast.6, s32[2,64]{1,0:T(2,128)} %bitcast.7, bf16[1728,256]{1,0:T(8,128)(2,1)} %bitcast.4), custom_call_target="tpu_custom_call" | custom-call | tf_op jit(solution)/shard_map/factor_solve/pallas_call | solution.py:439
  22.5 0.7 %copy.6 = f32[256,256]{1,0:T(8,128)} copy(f32[256,256]{1,0:T(8,128)S(1)} %factor_solve.1) | data formatting | bytes 524288
